TPU v7x, 256 devices: a whole 4x4x8 slice. The times are simulated.
256 devices in a mesh: ctx: 64 (over x_hi, z, y), head: 4 (over x_lo, core).
Axes of the slice: x: 4 (x_hi: 2, x_lo: 2; x = x_hi * 2 + x_lo), y: 4, z: 8, core: 2. Of those that a mesh axis runs over, the one named last changes fastest.
Arguments:
- queries: bfloat16 [8192, 4096], P('ctx', 'head'), may hold values from -81 to 81
- key_states: bfloat16 [8192, 1024], P('ctx', 'head'), may hold values from -7 to 7
- value_states: bfloat16 [8192, 1024], P('ctx', 'head'), may hold values from -6 to 6
- out_weight: bfloat16 [4096, 4096], P('head'), may hold values from -0.09375 to 0.09375
- head_role: int32 [8], replicated, may hold values from 0 to 1, as said below
- sink_len: int32 [8], replicated, may hold values from 32 to 128, as said below
- window_len: int32 [8], replicated, may hold values from 256 to 1024, as said below
Outputs:
- mixed: bfloat16 [8192, 4096], P(('ctx', 'head'))
Inputs may be any that keep to these rules, and one draw needn't show every extreme that they name: `head_role`: exactly 4 heads are retrieval heads. `sink_len`: some head has exactly 128. `window_len`: some head has exactly 1024.
All inputs are finite; a program needn't handle non-finite values.
Results may differ from a plain program's by a relative error of at most 0.012.
Values may be sent and summed in bfloat16 or wider, within the bound.
A program may use at most 128 MiB of HBM per device.

v0:
```python
import jax
import jax.numpy as jnp
from jax import lax
from jax.sharding import PartitionSpec as P

HD = 128
GROUP = 4
NEGATIVE = -1e30


def online_update(running, query_heads, key_part, value_part, allowed):
    row_peak, row_total, weighted = running
    scores = jnp.einsum(
        "thgd,jhd->thgj", query_heads, key_part, preferred_element_type=jnp.float32
    ) * HD ** (-0.5)
    visible = allowed[:, :, None, :]
    block_peak = jnp.max(jnp.where(visible, scores, NEGATIVE), axis=-1)
    new_peak = jnp.maximum(row_peak, block_peak)
    weights = jnp.where(visible, jnp.exp(scores - new_peak[..., None]), 0.0)
    row_total = jnp.sum(weights, axis=-1)
    weighted = jnp.einsum(
        "thgj,jhd->thgd",
        weights.astype(jnp.bfloat16),
        value_part,
        preferred_element_type=jnp.float32,
    )
    return (new_peak, row_total, weighted)


def empty_state(row_count, head_count):
    return (
        jnp.full((row_count, head_count, GROUP), NEGATIVE, jnp.float32),
        jnp.zeros((row_count, head_count, GROUP), jnp.float32),
        jnp.zeros((row_count, head_count, GROUP, HD), jnp.float32),
    )


def finish(running, row_count):
    row_peak, row_total, weighted = running
    return (weighted / row_total[..., None]).astype(jnp.bfloat16).reshape(row_count, -1)


def per_device(queries, key_states, value_states, out_weight, head_role, sink_len, window_len):
    row_count = queries.shape[0]
    local_heads = key_states.shape[1] // HD
    row_base = lax.axis_index("ctx") * row_count
    query_pos = row_base + jnp.arange(row_count, dtype=jnp.int32)
    my_group = lax.axis_index("head")
    first_head = my_group * local_heads
    last_row = row_base + row_count - 1
    roles_here = lax.dynamic_slice_in_dim(head_role, first_head, local_heads)
    sinks_here = lax.dynamic_slice_in_dim(sink_len, first_head, local_heads)
    windows_here = lax.dynamic_slice_in_dim(window_len, first_head, local_heads)
    query_heads = queries.reshape(row_count, local_heads, GROUP, HD)
    width = key_states.shape[1]
    both = lax.all_gather(
        jnp.concatenate([key_states, value_states], axis=1), "ctx", axis=0, tiled=True
    )
    key_part = both[:, :width].reshape(-1, local_heads, HD)
    value_part = both[:, width:].reshape(-1, local_heads, HD)
    key_pos = jnp.arange(key_part.shape[0], dtype=jnp.int32)

    def update(state):
        later = query_pos[:, None, None]
        earlier = key_pos[None, None, :]
        allowed = (earlier <= later) & (
            (roles_here[None, :, None] == 1)
            | (earlier < sinks_here[None, :, None])
            | (later - earlier < windows_here[None, :, None])
        )
        return online_update(state, query_heads, key_part, value_part, allowed)

    def unchanged(state):
        return state

    running = lax.cond(
        jnp.int32(0) <= last_row, update, unchanged, empty_state(row_count, local_heads)
    )
    attended = finish(running, row_count)
    mixed = lax.psum_scatter(
        jnp.dot(attended, out_weight, preferred_element_type=jnp.float32).astype(jnp.bfloat16),
        "head",
        scatter_dimension=0,
        tiled=True,
    )
    return mixed


def solution(mesh):
    in_specs = (
        P("ctx", "head"),
        P("ctx", "head"),
        P("ctx", "head"),
        P("head", None),
        P(),
        P(),
        P(),
    )
    out_specs = P(("ctx", "head"), None)
    return jax.shard_map(
        per_device, mesh=mesh, in_specs=in_specs, out_specs=out_specs, check_vma=False
    )
```

profile of v0, /device:TPU:1, one launch (start us, length us, event | category | flops | bytes accessed | tf_op | source)
XLA Modules:
  0.0 275.3 jit_solution(8369988572290120255)
XLA Ops:
  6.5 0.0 all-gather.2.cloned.1.call-start
  6.5 0.9 copy.27
  7.5 1.0 copy.28
  8.5 0.7 pad_maximum_fusion
  9.1 0.0 all-gather.2.cloned.1.call-update
  9.1 0.0 reduce-scatter.2.cloned.1.call-start
  9.2 173.6 %all-gather.2.cloned.1.call-done = bf16[8192,512]{0,1:T(8,128)(2,1)} async-done(((bf16[128,512]{0,1:T(8,128)(2,1)}), bf16[8192,512]{0,1:T(8,128)(2,1)}) %all-gather.2.cloned.1.call-update) | async-done | bytes 8388624 | tf_op jit(solution)/shard_map/all_gather | solution.py:56
  182.8 57.6 %conditional.1 = (f32[128,2,4]{0,2,1:T(4,128)S(1)}, f32[128,2,4,128]{0,3,2,1:T(8,128)S(1)}) conditional(s32[]{:T(128)} %convert_element_type.15, () %tuple.22, (s32[8192]{0:T(1024)S(1)}, s32[8192]{0:T(1024)S(1)}, s32[]{:T(128)}, s32[128]{0:T(128)S(1)}, s32[]{:T(128)}, /*index=5*/s32[8]{0:T(128)}, s32[8192]{0:T(1024)S(1)}, s32[8]{0:T(128)}, ...), branch_computations={%region_0.0_spmd, %region_1.4_spmd} | conditional | flops 4395662336 | bytes 180775088 | solution.py:76
  182.8 0.7 dynamic-slice_compare_fusion
  183.6 0.7 dynamic_slice.19
  184.3 0.7 dynamic_slice.20
  185.0 0.1 compare_or_fusion
  185.1 1.1 reshape.126
  186.2 0.0 copy-start
  186.3 3.7 %broadcast_compare_fusion = pred[128,8192]{0,1:T(8,128)(4,1)S(1)} fusion(s32[128]{0:T(128)S(1)} %broadcast_add_fusion, s32[8192]{0:T(1024)S(1)} %get-tuple-element.122), kind=kLoop, calls=%fused_computation.11 | loop fusion | flops 1048576 | bytes 1081856 | tf_op jit(solution)/shard_map/cond/branch_1_fun/le | solution.py:66
  190.0 1.2 broadcast_subtract_fusion
  191.2 2.8 %or_and_fusion = pred[128,2,8192]{0,2,1:T(8,128)(4,1)S(1)} fusion(s32[128,8192]{0,1:T(8,128)S(1)} %broadcast_subtract_fusion, s32[2]{0:T(128)S(1)} %dynamic_slice.20, pred[2,8192]{1,0:T(4,128)(4,1)S(1)} %compare_or_fusion, pred[128,8192]{0,1:T(8,128)(4,1)S(1)} %broadcast_compare_fusion), kind=kLoop, calls=%fused_computation.9 | loop fusion | flops 6291456 | bytes 7356424 | tf_op jit(solution)/shard_map/cond/branch_1_fun/and | solution.py:66
  194.0 0.0 copy-done
  194.1 2.3 fusion.15
  196.3 13.6 %fusion = (f32[128,2,4]{0,2,1:T(4,128)S(1)}, f32[2,8192,128,4]{2,1,3,0:T(8,128)}) fusion(pred[128,2,8192]{0,2,1:T(8,128)(4,1)S(1)} %or_and_fusion, bf16[8192,2,128,1]{0,2,3,1:T(8,128)(2,1)S(1)} %bitcast.33, bf16[128,2,4,128]{3,2,1,0:T(4,128)(2,1)S(1)} %reshape.126), kind=kOutput, calls=%fused_computation.2 | convolution fusion | flops 2172648448 | bytes 40112128 | tf_op jit(solution)/shard_map/cond/branch_1_fun/thgd,jhd->thgj/dot_general | solution.py:13
  209.9 15.9 %fusion.8 = f32[128,2,4,128]{3,0,2,1:T(8,128)S(1)} fusion(bf16[8192,2,128,1]{0,2,3,1:T(8,128)(2,1)} %bitcast.34, f32[2,8192,128,4]{2,1,3,0:T(8,128)} %get-tuple-element.144, f32[128,2,4]{0,2,1:T(4,128)S(1)} %broadcast_maximum_fusion, pred[128,2,8192]{0,2,1:T(8,128)(4,1)S(1)} %or_and_fusion), kind=kOutput, calls=%fused_computation.12 | convolution fusion | flops 2181038080 | bytes 40374272 | tf_op jit(solution)/shard_map/cond/branch_1_fun/thgj,jhd->thgd/dot_general | solution.py:21
  225.8 14.4 %fusion.4 = f32[128,2,4]{0,2,1:T(4,128)S(1)} fusion(f32[2,8192,128,4]{2,1,3,0:T(8,128)} %get-tuple-element.144, f32[128,2,4]{0,2,1:T(4,128)S(1)} %broadcast_maximum_fusion, pred[128,2,8192]{0,2,1:T(8,128)(4,1)S(1)} %or_and_fusion), kind=kLoop, calls=%fused_computation.6 | loop fusion | flops 33553408 | bytes 35659776 | tf_op jit(solution)/shard_map/cond/branch_1_fun/reduce_sum | solution.py:20
  240.2 0.2 copy.38
  240.4 0.1 divide_convert_fusion
  240.4 5.7 %convolution_convert_fusion = bf16[128,4096]{1,0:T(8,128)(2,1)} fusion(bf16[128,1024]{0,1:T(8,128)(2,1)S(1)} %bitcast.35, bf16[1024,4096]{1,0:T(8,128)(2,1)} %param.12), kind=kOutput, calls=%fused_computation.21 | convolution fusion | flops 1074266112 | bytes 9699328 | tf_op jit(solution)/shard_map/dot_general | solution.py:81
  246.1 0.0 reduce-scatter.2.cloned.1.call-update
  246.1 22.3 %reduce-scatter.2.cloned.1.call-done = bf16[32,4096]{1,0:T(8,128)(2,1)} async-done(((bf16[128,4096]{1,0:T(8,128)(2,1)}), bf16[32,4096]{1,0:T(8,128)(2,1)}) %reduce-scatter.2.cloned.1.call-update) | async-done | bytes 262160 | tf_op jit(solution)/shard_map/reduce_scatter | solution.py:80
  (4 shorter events, 0.0 us)
Async XLA Ops:
  6.5 176.3 %all-gather.2.cloned.1.call-start = ((), (), s32[]{:S(2)}) async-start(), calls=%async_computation.1 | async-start | bytes 8519680 | tf_op jit(solution)/shard_map/all_gather | solution.py:56
  9.1 259.3 %reduce-scatter.2.cloned.1.call-start = ((), (), s32[]{:S(2)}) async-start(), calls=%async_computation.2 | async-start | bytes 1310720 | tf_op jit(solution)/shard_map/reduce_scatter | solution.py:80
  186.2 7.8 %copy-start = (bf16[8192,512]{0,1:T(8,128)(2,1)S(1)}, bf16[8192,512]{0,1:T(8,128)(2,1)}, u32[]{:S(2)}) copy-start(bf16[8192,512]{0,1:T(8,128)(2,1)} %get-tuple-element.126) | copy-start | bytes 25165828 | tf_op jit(solution)/shard_map/cond
Sparse Core Ops, SparseCore 0:
  10.8 171.9 all-gather.1
  246.2 22.1 reduce-scatter.1
where the time goes:
time: 276 us; the launch traced here: 275 us
  waiting for transfers between devices  196 us (71%)
  matrix products  35.1 us (13%)
  other arithmetic  23.7 us (9%)
  between operations  13.4 us (5%)
  local copies, waits for them, and re-layouts  6.97 us (3%)
    all_gather x1, waiting for transfers between devices, per_device(): lax.all_gather(jnp.concatenate([key_states, value_states], axis=1), 'ctx'...  174 us
    reduce_scatter x1, waiting for transfers between devices, per_device(): lax.psum_scatter(jnp.dot(attended, out_weight, preferred_element_type=jnp...  22.3 us
    dot_general x1, matrix products, online_update(): jnp.einsum('thgj,jhd->thgd', weights.astype(jnp.bfloat16), value_part, pr...  15.9 us
    reduce_sum x1, other arithmetic, online_update(): row_total = jnp.sum(weights, axis=-1)  14.4 us
    dot_general x1, matrix products, online_update(): jnp.einsum('thgd,jhd->thgj', query_heads, key_part, preferred_element_typ...  13.6 us
    dot_general x1, matrix products, per_device(): jnp.dot(attended, out_weight, preferred_element_type=jnp.float32)  5.65 us
  transfers between devices with their start and end apart: 2, of which 2 were waited for; matrix products, arithmetic and copies ran while one was open for 0% of the time, Pallas kernels for 0%

commit v1 on v0

--- a/solution.py
+++ b/solution.py
@@ -53,9 +53,14 @@
     windows_here = lax.dynamic_slice_in_dim(window_len, first_head, local_heads)
     query_heads = queries.reshape(row_count, local_heads, GROUP, HD)
     width = key_states.shape[1]
-    both = lax.all_gather(
-        jnp.concatenate([key_states, value_states], axis=1), "ctx", axis=0, tiled=True
+    my_data = jnp.concatenate([key_states, value_states], axis=1)
+    prior = lax.all_to_all(
+        jnp.stack([my_data for _ in range(lax.axis_size("ctx"))], axis=0),
+        axis_name="ctx",
+        split_axis=0,
+        concat_axis=0,
     )
+    both = jnp.concatenate(prior, axis=0)
     key_part = both[:, :width].reshape(-1, local_heads, HD)
     value_part = both[:, width:].reshape(-1, local_heads, HD)
     key_pos = jnp.arange(key_part.shape[0], dtype=jnp.int32)

time: 276 us -> 314 us (1.14)
  starting transfers between devices: 0.04 us -> 15.7 us
  local copies, waits for them, and re-layouts: 6.97 us -> 19.6 us
  waiting for transfers between devices: 196 us -> 205 us
    all_to_all x0 -> x1, waiting for transfers between devices: none -> 183 us  [per_device(): lax.all_to_all(jnp.stack([my_data for _ in range(lax.axis_size('ctx'))],...]
    all_gather x1 -> x0, waiting for transfers between devices: 174 us -> none  [per_device(): lax.all_gather(jnp.concatenate([key_states, value_states], axis=1), 'ctx'...]
    all_to_all x0 -> x1, starting transfers between devices: none -> 15.5 us  [per_device(): lax.all_to_all(jnp.stack([my_data for _ in range(lax.axis_size('ctx'))],...]
    reshape x0 -> x1, local copies, waits for them, and re-layouts: none -> 7.84 us  [per_device(): both = jnp.concatenate(prior, axis=0)]
    another operation x0 -> x1, local copies, waits for them, and re-layouts: none -> 5.25 us  [per_device(): jnp.stack([my_data for _ in range(lax.axis_size('ctx'))], axis=0)]
where the time goes in v1:
time: 314 us
  waiting for transfers between devices  205 us (65%)
  matrix products  35.1 us (11%)
  other arithmetic  24.3 us (8%)
  local copies, waits for them, and re-layouts  19.6 us (6%)
  starting transfers between devices  15.7 us (5%)
  between operations  13.5 us (4%)
    all_to_all x1, waiting for transfers between devices, per_device(): lax.all_to_all(jnp.stack([my_data for _ in range(lax.axis_size('ctx'))],...  183 us
    reduce_scatter x1, waiting for transfers between devices, per_device(): lax.psum_scatter(jnp.dot(attended, out_weight, preferred_element_type=jnp...  22.8 us
    dot_general x1, matrix products, online_update(): jnp.einsum('thgj,jhd->thgd', weights.astype(jnp.bfloat16), value_part, pr...  15.9 us
    all_to_all x1, starting transfers between devices, per_device(): lax.all_to_all(jnp.stack([my_data for _ in range(lax.axis_size('ctx'))],...  15.5 us
    reduce_sum x1, other arithmetic, online_update(): row_total = jnp.sum(weights, axis=-1)  14.4 us
    dot_general x1, matrix products, online_update(): jnp.einsum('thgd,jhd->thgj', query_heads, key_part, preferred_element_typ...  13.5 us
    reshape x1, local copies, waits for them, and re-layouts, per_device(): both = jnp.concatenate(prior, axis=0)  7.84 us
  transfers between devices with their start and end apart: 2, of which 2 were waited for; matrix products, arithmetic and copies ran while one was open for 0% of the time, Pallas kernels for 0%

profile of v1, /device:TPU:1, one launch (start us, length us, event | category | flops | bytes accessed | tf_op | source)
XLA Modules:
  0.0 313.7 jit_solution(2997313566743088059)
XLA Ops:
  6.5 0.9 pad_maximum_fusion
  7.4 0.1 copy.26
  7.5 5.2 %stack.2 = bf16[64,128,512]{1,2,0:T(8,128)(2,1)} broadcast(bf16[128,512]{0,1:T(8,128)(2,1)S(1)} %copy.26), dimensions={1,2} | broadcast | bytes 8519680 | tf_op jit(solution)/shard_map/stack | solution.py:58
  12.8 0.0 copy-start
  12.8 0.0 copy-start.1
  12.8 0.0 copy-start.3
  12.8 15.5 %all-to-all-start = ((bf16[64,128,512]{1,2,0:T(8,128)(2,1)}), bf16[64,128,512]{1,2,0:T(8,128)(2,1)}, u32[]{:S(2)}, u32[]{:S(2)}) async-start(bf16[64,128,512]{1,2,0:T(8,128)(2,1)} %stack.2), calls=%async_computation | async-start | bytes 16777216 | tf_op jit(solution)/shard_map/all_to_all | solution.py:57
  28.3 0.2 reduce-scatter.2.cloned.1.call-start
  28.6 182.6 %all-to-all-done = bf16[64,128,512]{1,2,0:T(8,128)(2,1)} async-done(((bf16[64,128,512]{1,2,0:T(8,128)(2,1)}), bf16[64,128,512]{1,2,0:T(8,128)(2,1)}, u32[]{:S(2)}, u32[]{:S(2)}) %all-to-all-start) | async-done | bytes 8388640 | tf_op jit(solution)/shard_map/all_to_all | solution.py:57
  211.1 0.0 copy-done
  211.1 0.0 copy-done.1
  211.2 0.0 copy-done.2
  211.2 0.0 copy-done.3
  211.2 66.1 %conditional.1 = (f32[128,2,4]{0,2,1:T(4,128)S(1)}, f32[128,2,4,128]{0,3,2,1:T(8,128)}) conditional(s32[]{:T(128)} %convert_element_type.15, () %tuple.23, (s32[8192]{0:T(1024)S(1)}, s32[8192]{0:T(1024)S(1)}, s32[]{:T(128)}, s32[128]{0:T(128)S(1)}, s32[]{:T(128)}, /*index=5*/s32[8]{0:T(128)S(1)}, s32[8192]{0:T(1024)S(1)}, s32[8]{0:T(128)S(1)}, ...), branch_computations={%region_0.0_spmd, %region_1.4_spmd} | conditional | flops 4395662336 | bytes 163997840 | solution.py:81
  211.2 0.1 dynamic_slice.20
  211.3 0.1 dynamic_slice.19
  211.4 0.1 dynamic-slice_compare_fusion
  211.4 0.1 compare_or_fusion
  211.6 0.2 reshape.134
  211.7 3.7 %broadcast_compare_fusion = pred[128,8192]{0,1:T(8,128)(4,1)S(1)} fusion(s32[128]{0:T(128)S(1)} %broadcast_add_fusion, s32[8192]{0:T(1024)S(1)} %get-tuple-element.119), kind=kLoop, calls=%fused_computation.12 | loop fusion | flops 1048576 | bytes 1081856 | tf_op jit(solution)/shard_map/cond/branch_1_fun/le | solution.py:71
  215.5 1.2 broadcast_subtract_fusion
  216.7 2.8 or_and_fusion
  219.5 7.8 %copy_bitcast_fusion = bf16[8192,512]{0,1:T(8,128)(2,1)} fusion(bf16[64,128,512]{1,2,0:T(8,128)(2,1)} %get-tuple-element.146), kind=kLoop, calls=%fused_computation.9 | loop fusion | bytes 16777216 | tf_op jit(solution)/shard_map/reshape | solution.py:63
  227.4 5.1 %fusion.15 = (bf16[8192,256]{0,1:T(8,128)(2,1)}, bf16[8192,256]{0,1:T(8,128)(2,1)S(1)}) fusion(bf16[8192,512]{0,1:T(8,128)(2,1)} %copy_bitcast_fusion), kind=kLoop, calls=%fused_computation.25 | loop fusion | bytes 16777216 | tf_op jit(solution)/shard_map/slice | solution.py:65
  232.4 13.5 %fusion = (f32[128,2,4]{0,2,1:T(4,128)S(1)}, f32[2,8192,128,4]{2,1,3,0:T(8,128)}) fusion(pred[128,2,8192]{0,2,1:T(8,128)(4,1)S(1)} %or_and_fusion, bf16[8192,2,128,1]{0,2,3,1:T(8,128)(2,1)S(1)} %bitcast.38, bf16[128,2,4,128]{3,2,1,0:T(4,128)(2,1)S(1)} %reshape.134), kind=kOutput, calls=%fused_computation.2 | convolution fusion | flops 2172648448 | bytes 40112128 | tf_op jit(solution)/shard_map/cond/branch_1_fun/thgd,jhd->thgj/dot_general | solution.py:13
  246.0 15.9 %fusion.8 = f32[128,2,4,128]{3,0,2,1:T(8,128)S(1)} fusion(bf16[8192,2,128,1]{0,2,3,1:T(8,128)(2,1)} %bitcast.39, f32[2,8192,128,4]{2,1,3,0:T(8,128)} %get-tuple-element.152, f32[128,2,4]{0,2,1:T(4,128)S(1)} %broadcast_maximum_fusion, pred[128,2,8192]{0,2,1:T(8,128)(4,1)S(1)} %or_and_fusion), kind=kOutput, calls=%fused_computation.13 | convolution fusion | flops 2181038080 | bytes 40374272 | tf_op jit(solution)/shard_map/cond/branch_1_fun/thgj,jhd->thgd/dot_general | solution.py:21
  261.9 14.4 %fusion.4 = f32[128,2,4]{0,2,1:T(4,128)S(1)} fusion(f32[2,8192,128,4]{2,1,3,0:T(8,128)} %get-tuple-element.152, f32[128,2,4]{0,2,1:T(4,128)S(1)} %broadcast_maximum_fusion, pred[128,2,8192]{0,2,1:T(8,128)(4,1)S(1)} %or_and_fusion), kind=kLoop, calls=%fused_computation.6 | loop fusion | flops 33553408 | bytes 35659776 | tf_op jit(solution)/shard_map/cond/branch_1_fun/reduce_sum | solution.py:20
  276.3 1.0 copy.37
  277.3 1.1 divide_convert_fusion
  278.4 5.6 %convolution_convert_fusion = bf16[128,4096]{1,0:T(8,128)(2,1)} fusion(bf16[128,1024]{0,1:T(8,128)(2,1)S(1)} %bitcast.40, bf16[1024,4096]{1,0:T(8,128)(2,1)} %param.12), kind=kOutput, calls=%fused_computation.22 | convolution fusion | flops 1074266112 | bytes 9699328 | tf_op jit(solution)/shard_map/dot_general | solution.py:86
  284.0 0.0 reduce-scatter.2.cloned.1.call-update
  284.0 22.8 %reduce-scatter.2.cloned.1.call-done = bf16[32,4096]{1,0:T(8,128)(2,1)} async-done(((bf16[128,4096]{1,0:T(8,128)(2,1)}), bf16[32,4096]{1,0:T(8,128)(2,1)}) %reduce-scatter.2.cloned.1.call-update) | async-done | bytes 262160 | tf_op jit(solution)/shard_map/reduce_scatter | solution.py:85
  (5 shorter events, 0.0 us)
Async XLA Ops:
  12.8 198.4 %copy-start = (bf16[128,1024]{1,0:T(8,128)(2,1)S(1)}, bf16[128,1024]{1,0:T(8,128)(2,1)}, u32[]{:S(2)}) copy-start(bf16[128,1024]{1,0:T(8,128)(2,1)} %param.9) | copy-start | bytes 786436
  12.8 198.4 %copy-start.1 = (s32[8]{0:T(128)S(1)}, s32[8]{0:T(128)}, u32[]{:S(2)}) copy-start(s32[8]{0:T(128)} %param.13) | copy-start | bytes 100
  12.8 198.4 %copy-start.2 = (s32[8]{0:T(128)S(1)}, s32[8]{0:T(128)}, u32[]{:S(2)}) copy-start(s32[8]{0:T(128)} %param.14) | copy-start | bytes 100
  12.8 198.4 %copy-start.3 = (s32[8]{0:T(128)S(1)}, s32[8]{0:T(128)}, u32[]{:S(2)}) copy-start(s32[8]{0:T(128)} %param.15) | copy-start | bytes 100
  12.8 198.3 %all-to-all-start = ((bf16[64,128,512]{1,2,0:T(8,128)(2,1)}), bf16[64,128,512]{1,2,0:T(8,128)(2,1)}, u32[]{:S(2)}, u32[]{:S(2)}) async-start(bf16[64,128,512]{1,2,0:T(8,128)(2,1)} %stack.2), calls=%async_computation | async-start | bytes 16777216 | tf_op jit(solution)/shard_map/all_to_all | solution.py:57
  28.3 278.5 %reduce-scatter.2.cloned.1.call-start = ((), (), s32[]{:S(2)}) async-start(), calls=%async_computation.2 | async-start | bytes 1310720 | tf_op jit(solution)/shard_map/reduce_scatter | solution.py:85
Sparse Core Ops, SparseCore 0:
  284.2 22.6 reduce-scatter.1
